TPU v7x, 512 devices: a whole 4x4x16 slice. The times are simulated.
512 devices in a mesh: dp: 16 (over z), retr: 8 (over x, core), fsdp: 4 (over y).
Axes of the slice: x: 4, y: 4, z: 16, core: 2. Of those that a mesh axis runs over, the one named last changes fastest.
Arguments:
- queries: bfloat16 [65536, 2048], P(('dp', 'retr', 'fsdp')), may hold values from -110 to 110, as said below
- encodings: bfloat16 [2048, 128, 896], P(('dp', 'retr', 'fsdp')), may hold values from -6 to 6
- owner_ids: int32 [1024, 2], P(('dp', 'retr', 'fsdp')), may hold values from 0 to 7, all different within a row; in each aligned block of 2 rows (0 to 1, 2 to 3, ...) at most 2 rows name the same one
- local_ids: int32 [1024, 2], P(('dp', 'retr', 'fsdp')), may hold values from 0 to 3
- key_weight: bfloat16 [896, 2048], P(('dp', 'fsdp')), may hold values from -0.1875 to 0.1875
- value_weight: bfloat16 [896, 2048], P(('dp', 'fsdp')), may hold values from -0.1875 to 0.1875
Outputs:
- attended: bfloat16 [65536, 2048], P(('dp', 'retr', 'fsdp'))
Inputs may be any that keep to these rules, and one draw needn't show every extreme that they name: `queries`: entries are bounded. `owner_ids`: the two neighbours of a stretch have different owners; among the stretches of one device no owner is named more than 2 times, and in every draw some device's stretches name some owner exactly 2 times.
All inputs are finite; a program needn't handle non-finite values.
Results may differ from a plain program's by a relative error of at most 0.011.
Values may be sent and summed in bfloat16 or wider, within the bound.
No kernel may reach another device: no remote copies, remote signals or barrier semaphores. Data moves between devices by JAX's collectives and lax.ppermute only.
A program may use at most 64 MiB of HBM per device.

v0:
```python
import math
import jax
import jax.numpy as jnp
from jax import lax
from jax.sharding import PartitionSpec as P

HEADS = 16
STRETCH = 64


def passed_along(block, axis, distance):
    devices = range(lax.axis_size(axis))
    route = [(i - distance, i) for i in devices if i - distance in devices]
    return lax.ppermute(block, axis, route)


def body(queries, encodings, owner_ids, local_ids, key_weight, value_weight):
    tokens = queries.shape[0]
    columns = queries.shape[1]
    head_size = columns // HEADS
    stretches = tokens // STRETCH
    neighbours = owner_ids.shape[1]
    slot_count = stretches * neighbours
    owners = owner_ids.reshape(slot_count)
    places = local_ids.reshape(slot_count)
    gathered = lax.all_gather(encodings, "retr", axis=0, tiled=True)
    fetched = jnp.take(gathered, owners * encodings.shape[0] + places, axis=0)
    span = neighbours * encodings.shape[1]
    panel_rows = fetched.reshape(stretches * span, encodings.shape[2])
    key_full, value_full = (
        lax.all_gather(key_weight, ("dp", "fsdp"), axis=0, tiled=True),
        lax.all_gather(value_weight, ("dp", "fsdp"), axis=0, tiled=True),
    )
    prior_rows = passed_along(panel_rows[(stretches - 1) * span :], "fsdp", 1)
    every_row = jnp.concatenate([prior_rows, panel_rows], 0)
    key_block = jnp.dot(every_row, key_full, preferred_element_type=jnp.float32).astype(
        jnp.bfloat16
    )
    value_block = jnp.dot(every_row, value_full, preferred_element_type=jnp.float32).astype(
        jnp.bfloat16
    )
    key_block = key_block.reshape(stretches + 1, span, columns)
    value_block = value_block.reshape(stretches + 1, span, columns)
    padded = jnp.concatenate(
        [
            jnp.zeros((1, columns), jnp.bfloat16),
            queries,
            jnp.zeros((STRETCH - 1, columns), jnp.bfloat16),
        ],
        0,
    )
    query_block = padded.reshape(stretches + 1, STRETCH, HEADS, head_size)
    key_heads = key_block.reshape(stretches + 1, span, HEADS, head_size)
    value_heads = value_block.reshape(stretches + 1, span, HEADS, head_size)
    scores = jnp.einsum(
        "cqhd,ckhd->chqk", query_block, key_heads, preferred_element_type=jnp.float32
    ) / math.sqrt(head_size)
    probs = jax.nn.softmax(scores, axis=-1).astype(jnp.bfloat16)
    result = jnp.einsum(
        "chqk,ckhd->cqhd", probs, value_heads, preferred_element_type=jnp.float32
    ).astype(jnp.bfloat16)
    result = result.reshape((stretches + 1) * STRETCH, columns)[1 : tokens + 1]
    follower = lax.axis_index("fsdp") > 0
    position = jnp.arange(tokens, dtype=jnp.int32)
    visible = follower | (position >= STRETCH - 1)
    return jnp.where(visible[:, None], result, jnp.zeros_like(result))


def solution(mesh):
    in_specs = (
        P(("dp", "retr", "fsdp"), None),
        P(("dp", "retr", "fsdp"), None, None),
        P(("dp", "retr", "fsdp"), None),
        P(("dp", "retr", "fsdp"), None),
        P(("dp", "fsdp"), None),
        P(("dp", "fsdp"), None),
    )
    out_specs = P(("dp", "retr", "fsdp"), None)
    return jax.shard_map(body, mesh=mesh, in_specs=in_specs, out_specs=out_specs, check_vma=False)
```

profile of v0, /device:TPU:2, one launch (start us, length us, event | category | flops | bytes accessed | tf_op | source)
XLA Modules:
  0.0 400.2 jit_solution(17860496296428153999)
XLA Ops:
  6.5 0.7 all-gather.6.cloned.1.call-update
  7.3 0.7 all-gather.8.cloned.1.call-update
  8.1 0.7 all-gather.10.cloned.1.call-update
  8.7 0.7 multiply_add_fusion
  9.8 1.4 maximum_bitcast_fusion
  11.2 1.1 copy.17
  12.3 53.7 %all-gather.6.cloned.1.call-done = bf16[32,128,896]{2,1,0:T(8,128)(2,1)} async-done(((bf16[4,128,896]{2,1,0:T(8,128)(2,1)}), bf16[32,128,896]{2,1,0:T(8,128)(2,1)}) %all-gather.6.cloned.1.call-update) | async-done | bytes 7340048 | tf_op jit(solution)/shard_map/all_gather | solution.py:26
  66.0 3.8 gather_fusion
  69.9 3.4 collective-permute-start
  73.4 142.8 %all-gather.8.cloned.1.call-done = bf16[64,14,2048]{2,1,0:T(8,128)(2,1)} async-done(((bf16[1,14,2048]{2,1,0:T(8,128)(2,1)}), bf16[64,14,2048]{2,1,0:T(8,128)(2,1)}) %all-gather.8.cloned.1.call-update) | async-done | bytes 3670032 | tf_op jit(solution)/shard_map/all_gather | solution.py:32
  216.3 6.0 %reshape.73 = bf16[896,2048]{1,0:T(8,128)(2,1)} reshape(bf16[64,14,2048]{2,1,0:T(8,128)(2,1)} %all-gather.8.cloned.1.call-done) | data formatting | bytes 7340032
  222.2 137.9 %all-gather.10.cloned.1.call-done = bf16[64,14,2048]{2,1,0:T(8,128)(2,1)} async-done(((bf16[1,14,2048]{2,1,0:T(8,128)(2,1)}), bf16[64,14,2048]{2,1,0:T(8,128)(2,1)}) %all-gather.10.cloned.1.call-update) | async-done | bytes 3670032 | tf_op jit(solution)/shard_map/all_gather | solution.py:31
  360.1 6.0 %reshape.75 = bf16[896,2048]{1,0:T(8,128)(2,1)} reshape(bf16[64,14,2048]{2,1,0:T(8,128)(2,1)} %all-gather.10.cloned.1.call-done) | data formatting | bytes 7340032
  366.2 0.2 bitcast_select_fusion
  366.4 6.0 %fusion.8 = bf16[96,8,16,128]{3,1,2,0:T(8,128)(2,1)S(1)} fusion(bf16[896,2048]{1,0:T(8,128)(2,1)} %reshape.73, bf16[512,896]{1,0:T(8,128)(2,1)S(1)} %bitcast_select_fusion, bf16[256,896]{1,0:T(8,128)(2,1)S(1)} %collective-permute-done), kind=kOutput, calls=%fused_computation.12 | convolution fusion | flops 2822897664 | bytes 8192000 | tf_op jit(solution)/shard_map/dot_general | solution.py:39
  372.5 2.7 copy.19
  375.2 4.0 fusion.9
  379.1 1.0 copy.18
  380.3 1.2 fusion.3
  381.5 1.1 fusion.30
  382.6 8.2 %fusion.15 = bf16[3,64,16,128]{3,1,2,0:T(8,128)(2,1)} fusion(bf16[3,256,16,128]{3,2,1,0:T(8,128)(2,1)} %bitcast.33, f32[3,16,64]{2,1,0:T(8,128)S(1)} %fusion.30, f32[3,16,64,256]{3,2,1,0:T(8,128)S(1)} %fusion.3), kind=kOutput, calls=%fused_computation.18 | convolution fusion | flops 205655296 | bytes 7090176 | tf_op jit(solution)/shard_map/chqk,ckhd->cqhd/dot_general | solution.py:59
  390.9 1.6 copy.16
  392.5 0.2 copy.32
  392.7 1.0 slice_select_fusion
  (20 shorter events, 0.7 us)
Async XLA Ops:
  6.5 59.5 %all-gather.6.cloned.1.call-start = ((), (), s32[]{:S(2)}) async-start(), calls=%async_computation | async-start | bytes 8257536 | tf_op jit(solution)/shard_map/all_gather | solution.py:26
  7.3 209.0 %all-gather.8.cloned.1.call-start = ((), (), s32[]{:S(2)}) async-start(), calls=%async_computation.1 | async-start | bytes 4259840 | tf_op jit(solution)/shard_map/all_gather | solution.py:32
  8.0 352.1 %all-gather.10.cloned.1.call-start = ((), (), s32[]{:S(2)}) async-start(), calls=%async_computation.2 | async-start | bytes 4259840 | tf_op jit(solution)/shard_map/all_gather | solution.py:31
  69.9 296.5 %collective-permute-start = (bf16[256,896]{1,0:T(8,128)(2,1)S(1)}, bf16[256,896]{1,0:T(8,128)(2,1)S(1)}, u32[]{:S(2)}, u32[]{:S(2)}) collective-permute-start(bf16[256,896]{1,0:T(8,128)(2,1)S(1)} %bitcast.36), channel_id=1, source_target_pairs={{0,1},{1,2},{2,3},{4,5},{5,6},{6,7},{8,9},{9,10},{10,11},{12,13},{... | collective-permute-start | bytes 1376264 | tf_op jit(solution)/shard_map/ppermute | solution.py:14
  372.5 2.7 copy-start
  379.1 1.1 copy-start.1
Sparse Core Ops, SparseCore 0:
  9.5 56.5 all-gather.5
  68.9 147.2 all-gather.7
  219.2 140.8 all-gather.9
where the time goes:
time: 401 us; the launch traced here: 400 us
  waiting for transfers between devices  337 us (84%)
  local copies, waits for them, and re-layouts  22.9 us (6%)
  matrix products  19.5 us (5%)
  between operations  13.2 us (3%)
  other arithmetic  4.63 us (1%)
    all_gather x1, waiting for transfers between devices, body(): lax.all_gather(value_weight, ('dp', 'fsdp'), axis=0, tiled=True)  143 us
    all_gather x1, waiting for transfers between devices, body(): lax.all_gather(key_weight, ('dp', 'fsdp'), axis=0, tiled=True)  138 us
    all_gather x1, waiting for transfers between devices, body(): gathered = lax.all_gather(encodings, 'retr', axis=0, tiled=True)  53.7 us
    unnamed x10, local copies, waits for them, and re-layouts  17.1 us
    dot_general x1, matrix products, body(): jnp.einsum('chqk,ckhd->cqhd', probs, value_heads, preferred_element_type=...  8.23 us
  transfers between devices with their start and end apart: 4, of which 3 were waited for; matrix products, arithmetic and copies ran while one was open for 5% of the time, Pallas kernels for 0%

commit v1 on v0

--- a/solution.py
+++ b/solution.py
@@ -29,7 +29,12 @@
     panel_rows = fetched.reshape(stretches * span, encodings.shape[2])
     key_full, value_full = (
         lax.all_gather(key_weight, ("dp", "fsdp"), axis=0, tiled=True),
-        lax.all_gather(value_weight, ("dp", "fsdp"), axis=0, tiled=True),
+        jnp.concatenate(
+            lax.all_to_all(
+                jnp.stack([value_weight] * lax.axis_size(("dp", "fsdp"))), ("dp", "fsdp"), 0, 0
+            ),
+            axis=0,
+        ),
     )
     prior_rows = passed_along(panel_rows[(stretches - 1) * span :], "fsdp", 1)
     every_row = jnp.concatenate([prior_rows, panel_rows], 0)

time: 401 us -> 309 us (0.77)
  the two profiles are of different devices: /device:TPU:2 before, /device:TPU:16 now
where the time goes in v1:
time: 309 us; the launch traced here: 308 us
  waiting for transfers between devices  221 us (72%)
  local copies, waits for them, and re-layouts  27.2 us (9%)
  starting transfers between devices  22.1 us (7%)
  matrix products  21.5 us (7%)
  between operations  13.6 us (4%)
    all_gather x1, waiting for transfers between devices, body(): lax.all_gather(key_weight, ('dp', 'fsdp'), axis=0, tiled=True)  185 us
    all_gather x1, waiting for transfers between devices, body(): gathered = lax.all_gather(encodings, 'retr', axis=0, tiled=True)  34.5 us
    all_to_all x1, starting transfers between devices, body(): lax.all_to_all(jnp.stack([value_weight] * lax.axis_size(('dp', 'fsdp'))),...  18.9 us
    unnamed x17, local copies, waits for them, and re-layouts  12 us
    dot_general x1, matrix products, body(): jnp.einsum('chqk,ckhd->cqhd', probs, value_heads, preferred_element_type=...  8.23 us
  transfers between devices with their start and end apart: 4, of which 2 were waited for; matrix products, arithmetic and copies ran while one was open for 8% of the time, Pallas kernels for 0%

profile of v1, /device:TPU:16, one launch (start us, length us, event | category | flops | bytes accessed | tf_op | source)
XLA Modules:
  0.0 308.2 jit_solution(9500217518601196052)
XLA Ops:
  6.5 0.7 all-gather.4.cloned.1.call-update
  7.3 3.4 %stack.2 = bf16[64,14,2048]{2,1,0:T(8,128)(2,1)} broadcast(bf16[14,2048]{1,0:T(8,128)(2,1)} %param.11), dimensions={1,2} | broadcast | bytes 3727360 | tf_op jit(solution)/shard_map/stack | solution.py:34
  10.7 18.9 %all-to-all-start = ((bf16[64,14,2048]{2,1,0:T(8,128)(2,1)}), bf16[64,14,2048]{2,1,0:T(8,128)(2,1)}, u32[]{:S(2)}, u32[]{:S(2)}) async-start(bf16[64,14,2048]{2,1,0:T(8,128)(2,1)} %stack.2), calls=%async_computation | async-start | bytes 8388608 | tf_op jit(solution)/shard_map/all_to_all | solution.py:33
  29.7 0.7 all-gather.6.cloned.1.call-update
  30.7 0.4 maximum_bitcast_fusion
  31.1 1.1 copy.17
  32.2 34.5 %all-gather.4.cloned.1.call-done = bf16[32,128,896]{2,1,0:T(8,128)(2,1)} async-done(((bf16[4,128,896]{2,1,0:T(8,128)(2,1)}), bf16[32,128,896]{2,1,0:T(8,128)(2,1)}) %all-gather.4.cloned.1.call-update) | async-done | bytes 7340048 | tf_op jit(solution)/shard_map/all_gather | solution.py:26
  66.7 3.8 %gather_fusion = bf16[4,128,896]{2,1,0:T(8,128)(2,1)S(1)} fusion(bf16[32,128,896]{2,1,0:T(8,128)(2,1)} %all-gather.4.cloned.1.call-done, s32[1024]{0:T(1024)S(1)} %pad_clamp_fusion), kind=kCustom, calls=%fused_computation | custom fusion | bytes 1835024 | tf_op jit(solution)/shard_map/jit(_take)/gather | solution.py:27
  70.6 3.1 %collective-permute-start = (bf16[256,896]{1,0:T(8,128)(2,1)S(1)}, bf16[256,896]{1,0:T(8,128)(2,1)S(1)}, u32[]{:S(2)}, u32[]{:S(2)}) collective-permute-start(bf16[256,896]{1,0:T(8,128)(2,1)S(1)} %bitcast.35), channel_id=1, source_target_pairs={{0,1},{1,2},{2,3},{4,5},{5,6},{6,7},{8,9},{9,10},{10,11},{12,13},{... | collective-permute-start | bytes 1376264 | tf_op jit(solution)/shard_map/ppermute | solution.py:14
  73.8 185.1 %all-gather.6.cloned.1.call-done = bf16[64,14,2048]{2,1,0:T(8,128)(2,1)} async-done(((bf16[1,14,2048]{2,1,0:T(8,128)(2,1)}), bf16[64,14,2048]{2,1,0:T(8,128)(2,1)}) %all-gather.6.cloned.1.call-update) | async-done | bytes 3670032 | tf_op jit(solution)/shard_map/all_gather | solution.py:31
  258.9 6.0 %reshape.79 = bf16[896,2048]{1,0:T(8,128)(2,1)} reshape(bf16[64,14,2048]{2,1,0:T(8,128)(2,1)} %all-gather.6.cloned.1.call-done) | data formatting | bytes 7340032
  264.9 0.2 bitcast_select_fusion
  265.1 0.9 copy-done.1
  266.0 6.2 %fusion.9 = bf16[96,8,16,128]{3,1,2,0:T(8,128)(2,1)S(1)} fusion(bf16[896,2048]{1,0:T(8,128)(2,1)} %reshape.79, bf16[512,896]{1,0:T(8,128)(2,1)S(1)} %bitcast_select_fusion, bf16[256,896]{1,0:T(8,128)(2,1)S(1)} %collective-permute-done), kind=kOutput, calls=%fused_computation.13 | convolution fusion | flops 2822897664 | bytes 8192000 | tf_op jit(solution)/shard_map/dot_general | solution.py:41
  272.2 1.0 copy.18
  273.4 1.2 fusion.3
  274.6 1.1 fusion.30
  275.7 6.0 %reshape.67 = bf16[896,2048]{1,0:T(8,128)(2,1)} reshape(bf16[64,14,2048]{2,1,0:T(8,128)(2,1)} %all-to-all-done) | data formatting | bytes 7340032 | tf_op jit(solution)/shard_map/reshape | solution.py:32
  281.7 5.9 %fusion.8 = bf16[96,8,16,128]{3,1,2,0:T(8,128)(2,1)S(1)} fusion(bf16[896,2048]{1,0:T(8,128)(2,1)} %reshape.67, bf16[512,896]{1,0:T(8,128)(2,1)} %copy-done.1, bf16[256,896]{1,0:T(8,128)(2,1)} %copy-done.5), kind=kOutput, calls=%fused_computation.12 | convolution fusion | flops 2822897664 | bytes 8192000 | tf_op jit(solution)/shard_map/dot_general | solution.py:44
  287.6 2.7 copy.19
  290.3 8.2 %fusion.15 = bf16[3,64,16,128]{3,1,2,0:T(8,128)(2,1)} fusion(bf16[3,256,16,128]{3,2,1,0:T(8,128)(2,1)} %bitcast.32, f32[3,16,64]{2,1,0:T(8,128)S(1)} %fusion.30, f32[3,16,64,256]{3,2,1,0:T(8,128)S(1)} %fusion.3), kind=kOutput, calls=%fused_computation.18 | convolution fusion | flops 205655296 | bytes 7090176 | tf_op jit(solution)/shard_map/chqk,ckhd->cqhd/dot_general | solution.py:64
  298.5 1.6 copy.16
  300.2 0.2 copy.32
  300.4 1.0 slice_select_fusion
  (28 shorter events, 0.7 us)
Async XLA Ops:
  6.5 60.1 %all-gather.4.cloned.1.call-start = ((), (), s32[]{:S(2)}) async-start(), calls=%async_computation.1 | async-start | bytes 8257536 | tf_op jit(solution)/shard_map/all_gather | solution.py:26
  10.7 19.7 %copy-start.3 = (s32[2,2]{1,0:T(2,128)S(1)}, s32[2,2]{1,0:T(2,128)}, u32[]{:S(2)}) copy-start(s32[2,2]{1,0:T(2,128)} %param.9) | copy-start | bytes 52
  10.7 19.7 %copy-start.4 = (s32[2,2]{1,0:T(2,128)S(1)}, s32[2,2]{1,0:T(2,128)}, u32[]{:S(2)}) copy-start(s32[2,2]{1,0:T(2,128)} %param.8) | copy-start | bytes 52
  10.7 20.1 %copy-start.2 = (bf16[128,2048]{1,0:T(8,128)(2,1)S(1)}, bf16[128,2048]{1,0:T(8,128)(2,1)}, u32[]{:S(2)}) copy-start(bf16[128,2048]{1,0:T(8,128)(2,1)} %param.6) | copy-start | bytes 1572868
  10.7 265.1 %all-to-all-start = ((bf16[64,14,2048]{2,1,0:T(8,128)(2,1)}), bf16[64,14,2048]{2,1,0:T(8,128)(2,1)}, u32[]{:S(2)}, u32[]{:S(2)}) async-start(bf16[64,14,2048]{2,1,0:T(8,128)(2,1)} %stack.2), calls=%async_computation | async-start | bytes 8388608 | tf_op jit(solution)/shard_map/all_to_all | solution.py:33
  29.6 229.3 %all-gather.6.cloned.1.call-start = ((), (), s32[]{:S(2)}) async-start(), calls=%async_computation.2 | async-start | bytes 4259840 | tf_op jit(solution)/shard_map/all_gather | solution.py:31
  70.6 194.5 %collective-permute-start = (bf16[256,896]{1,0:T(8,128)(2,1)S(1)}, bf16[256,896]{1,0:T(8,128)(2,1)S(1)}, u32[]{:S(2)}, u32[]{:S(2)}) collective-permute-start(bf16[256,896]{1,0:T(8,128)(2,1)S(1)} %bitcast.35), channel_id=1, source_target_pairs={{0,1},{1,2},{2,3},{4,5},{5,6},{6,7},{8,9},{9,10},{10,11},{12,13},{... | collective-permute-start | bytes 1376264 | tf_op jit(solution)/shard_map/ppermute | solution.py:14
  265.1 0.9 copy-start.1
  266.0 6.2 %copy-start.5 = (bf16[256,896]{1,0:T(8,128)(2,1)}, bf16[256,896]{1,0:T(8,128)(2,1)S(1)}, u32[]{:S(2)}) copy-start(bf16[256,896]{1,0:T(8,128)(2,1)S(1)} %collective-permute-done) | copy-start | bytes 1376260
  272.2 1.1 copy-start
Sparse Core Ops, SparseCore 0:
  9.5 57.1 all-gather.3
  69.6 189.2 all-gather.5
